TPU v7x, 32 devices: a whole 2x2x4 slice. The times are simulated.
32 devices in a mesh: ctx: 16 (over z, y, core), head: 2 (over x).
Axes of the slice: x: 2, y: 2, z: 4, core: 2. Of those that a mesh axis runs over, the one named last changes fastest.
Arguments:
- query_gate: bfloat16 [4096, 4096], P(('ctx', 'head')), may hold values from -6 to 6
- key_gate: bfloat16 [4096, 4096], P(('ctx', 'head')), may hold values from -6 to 6
- values: bfloat16 [4096, 4096], P(('ctx', 'head')), may hold values from -6 to 6
- rate_mix: float32 [512, 8], replicated, may hold values from 0 to 1
- residue: float32 [512, 8], replicated, may hold values from -4.5 to 4.5
- skip_gain: float32 [4096], replicated, may hold values from 0.25 to 1.75
- doc_lengths: int32 [16], replicated, may hold values from 1 to 1024, 4096 in all
Outputs:
- gated_out: bfloat16 [4096, 4096], P(('ctx', 'head'))
Inputs may be any that keep to these rules, and one draw needn't show every extreme that they name: `doc_lengths`: the lengths sum to 4096, and the longest is exactly 1024.
All inputs are finite; a program needn't handle non-finite values.
Results may differ from a plain program's by a relative error of at most 0.014.
Values may be sent and summed in bfloat16 or wider, within the bound.
A program may use at most 64 MiB of HBM per device.

v0:
```python
import math

import jax
import jax.numpy as jnp
from jax import lax
from jax.sharding import PartitionSpec as P

BLOCK = 128


highest = lax.Precision.HIGHEST


def carried_in(shard, axis, combine, identity):
    devices, position = (lax.axis_size(axis), lax.axis_index(axis))
    everything = jax.tree.map(lambda part: lax.all_gather(part, axis), shard)
    start = jax.tree.map(
        lambda part, zero: jnp.broadcast_to(jnp.asarray(zero, part.dtype), part.shape),
        shard,
        identity,
    )

    def hop(k, before):
        reached = k < position
        new = combine(before, jax.tree.map(lambda part: part[k], everything))
        return jax.tree.map(lambda a, b: jnp.where(reached, a, b), new, before)

    return lax.fori_loop(0, devices, hop, start)


def doc_index(positions, doc_lengths):
    doc_ends = jnp.cumsum(doc_lengths)
    hits = (positions[:, None] >= doc_ends[None, :]).astype(jnp.int32)
    return jnp.sum(hits, axis=1)


def mode_tables(rate_mix, residue, total_tokens):
    decay_rate = jnp.exp(-math.log(30.0) - rate_mix * math.log(float(total_tokens)))
    weights = residue * jnp.sqrt(-jnp.expm1(-2.0 * decay_rate))
    return (decay_rate, weights)


def make_combine(decay_full):

    def combine(earlier, later):
        state_first, keep_first, length_first = earlier
        state_later, keep_later, length_later = later
        factor = keep_later * jnp.exp(-decay_full * length_later)
        return (
            factor * state_first + state_later,
            keep_first * keep_later,
            length_first + length_later,
        )

    return combine


def tile_conv(mixed_tile, doc_ids, doc_prev, decay_full, weight_full, carried):
    row_count = mixed_tile.shape[0]
    offsets = jnp.arange(row_count).astype(jnp.float32)
    allowed = (doc_ids[:, None] == doc_ids[None, :]) & (offsets[:, None] >= offsets[None, :])
    mask_matrix = allowed.astype(jnp.float32)
    linked = (doc_ids == doc_prev).astype(jnp.float32)
    mixed_float = mixed_tile.astype(jnp.float32)

    def per_mode(total, operands):
        rate_row, weight_row, carried_row = operands
        scaled = mixed_float * jnp.exp(rate_row[None, :] * offsets[:, None])
        inner_term = jnp.dot(
            mask_matrix, scaled, precision=highest, preferred_element_type=jnp.float32
        )
        outside = weight_row[None, :] * jnp.exp(-rate_row[None, :] * offsets[:, None])
        cross_term = linked[:, None] * (jnp.exp(-rate_row) * carried_row)[None, :]
        return (total + outside * (inner_term + cross_term), None)

    start_total = jnp.zeros(mixed_float.shape, jnp.float32)
    total, _ = lax.scan(per_mode, start_total, (decay_full, weight_full, carried))
    return total


def tile_state(mixed_tile, doc_ids, doc_prev, decay_full):
    row_count = mixed_tile.shape[0]
    offsets = jnp.arange(row_count).astype(jnp.float32)
    tail_mask = (doc_ids == doc_ids[row_count - 1]).astype(jnp.float32)
    masked = mixed_tile.astype(jnp.float32) * tail_mask[:, None]
    remaining = (row_count - 1 - offsets)[:, None]

    def per_mode(rate_row):
        return jnp.sum(jnp.exp(-rate_row[None, :] * remaining) * masked, axis=0)

    local_state = lax.map(per_mode, decay_full)
    keep_flag = (doc_ids[row_count - 1] == doc_prev).astype(jnp.float32)
    return (local_state, keep_flag)


def prepare(mixed, span_start, decay_full, doc_lengths):
    row_count = mixed.shape[0]
    tile_len = min(BLOCK, row_count)
    combine = make_combine(decay_full)
    pieces = []
    device_map = None
    for tile_index in range(row_count // tile_len):
        tile_start = span_start + tile_index * tile_len
        positions = tile_start + jnp.arange(tile_len, dtype=jnp.int32)
        doc_ids = doc_index(positions, doc_lengths)
        before = jnp.reshape(jnp.maximum(tile_start - 1, 0), (1,))
        doc_prev = doc_index(before, doc_lengths)[0]
        mixed_tile = mixed[tile_index * tile_len : (tile_index + 1) * tile_len]
        local_state, keep_flag = tile_state(mixed_tile, doc_ids, doc_prev, decay_full)
        element = (local_state, keep_flag, jnp.asarray(float(tile_len), jnp.float32))
        device_map = element if device_map is None else combine(device_map, element)
        pieces.append((mixed_tile, doc_ids, doc_prev, local_state, keep_flag))
    return (pieces, device_map)


def identity_of(device_map):
    return (jnp.zeros_like(device_map[0]), jnp.ones((), jnp.float32), jnp.zeros((), jnp.float32))


def finish(pieces, entering, decay_full, weight_full, skip_local):
    outputs = []
    carried = entering
    for mixed_tile, doc_ids, doc_prev, local_state, keep_flag in pieces:
        convolved = tile_conv(mixed_tile, doc_ids, doc_prev, decay_full, weight_full, carried)
        convolved = convolved + skip_local[None, :] * mixed_tile.astype(jnp.float32)
        outputs.append(convolved.astype(jnp.bfloat16))
        carried = keep_flag * jnp.exp(-decay_full * mixed_tile.shape[0]) * carried + local_state
    return jnp.concatenate(outputs, axis=0)


def widen(table, group_width):
    return jnp.repeat(table.T, group_width, axis=1)


def shards(query_gate, key_gate, values, rate_mix, residue, skip_gain, doc_lengths):
    ctx_count = lax.axis_size("ctx")
    head_count = lax.axis_size("head")
    tok_dev = query_gate.shape[0]
    total_tokens = tok_dev * ctx_count * head_count
    group_width = skip_gain.shape[0] // rate_mix.shape[0]
    decay_all, weight_all = mode_tables(rate_mix, residue, total_tokens)
    head_pos = lax.axis_index("head")
    group_local = rate_mix.shape[0] // head_count
    chan_local = skip_gain.shape[0] // head_count
    decay_rate = lax.dynamic_slice_in_dim(decay_all, head_pos * group_local, group_local, 0)
    weights = lax.dynamic_slice_in_dim(weight_all, head_pos * group_local, group_local, 0)
    skip_local = lax.dynamic_slice_in_dim(skip_gain, head_pos * chan_local, chan_local, 0)
    decay_full = widen(decay_rate, group_width)
    weight_full = widen(weights, group_width)
    span_start = lax.axis_index("ctx") * (tok_dev * head_count)
    query_part, key_part, value_part = (
        lax.all_to_all(query_gate, "head", split_axis=1, concat_axis=0, tiled=True),
        lax.all_to_all(key_gate, "head", split_axis=1, concat_axis=0, tiled=True),
        lax.all_to_all(values, "head", split_axis=1, concat_axis=0, tiled=True),
    )
    mixed = key_part * value_part
    pieces, device_map = prepare(mixed, span_start, decay_full, doc_lengths)
    entering = carried_in(device_map, "ctx", make_combine(decay_full), identity_of(device_map))[0]
    smoothed = finish(pieces, entering, decay_full, weight_full, skip_local)
    result = lax.all_to_all(query_part * smoothed, "head", split_axis=0, concat_axis=1, tiled=True)
    return result


def solution(mesh):
    return jax.shard_map(
        shards,
        mesh=mesh,
        in_specs=(
            P(("ctx", "head"), None),
            P(("ctx", "head"), None),
            P(("ctx", "head"), None),
            P(),
            P(),
            P(),
            P(),
        ),
        out_specs=P(("ctx", "head"), None),
        check_vma=False,
    )
```

profile of v0, /device:TPU:0, one launch (start us, length us, event | category | flops | bytes accessed | tf_op | source)
XLA Modules:
  0.0 235.4 jit_solution(10150110454636433883)
XLA Ops:
  6.5 2.3 copy.38
  8.8 4.4 %all-to-all-start.1 = ((bf16[128,2,2048]{0,2,1:T(8,128)(2,1)}), bf16[128,2,2048]{0,2,1:T(8,128)(2,1)S(1)}, u32[]{:S(2)}, u32[]{:S(2)}) async-start(bf16[128,2,2048]{0,2,1:T(8,128)(2,1)} %bitcast.4), calls=%async_computation.1 | async-start | bytes 2097152 | tf_op jit(solution)/shard_map/all_to_all | solution.py:153
  16.7 10.9 %all-to-all-done.1 = bf16[128,2,2048]{0,2,1:T(8,128)(2,1)S(1)} async-done(((bf16[128,2,2048]{0,2,1:T(8,128)(2,1)}), bf16[128,2,2048]{0,2,1:T(8,128)(2,1)S(1)}, u32[]{:S(2)}, u32[]{:S(2)}) %all-to-all-start.1) | async-done | bytes 1048608 | tf_op jit(solution)/shard_map/all_to_all | solution.py:153
  27.6 3.7 %all-to-all-start.2 = ((bf16[128,2,2048]{0,2,1:T(8,128)(2,1)}), bf16[128,2,2048]{0,2,1:T(8,128)(2,1)S(1)}, u32[]{:S(2)}, u32[]{:S(2)}) async-start(bf16[128,2,2048]{0,2,1:T(8,128)(2,1)} %bitcast.5), calls=%async_computation.2 | async-start | bytes 2097152 | tf_op jit(solution)/shard_map/all_to_all | solution.py:154
  33.6 3.3 %compare_convert_fusion.1 = (f32[128]{0:T(128)S(1)}, f32[128]{0:T(128)}, f32[128]{0:T(128)S(1)}, f32[128]{0:T(128)}) fusion(s32[128]{0:T(128)S(1)} %get-tuple-element.954, s32[]{:T(128)} %bitcast.9, s32[]{:T(128)} %get-tuple-element.538, s32[128]{0:T(128)S(1)} %get-tuple-element.921, s32[]{:T(128)} %bitcast.10, s32[]{:T(128)} %get-tuple-element.537), kind=kLoop, calls=%fused_computation.84 | loop fusion | flops 1024 | bytes 3088 | tf_op jit(solution)/shard_map/convert_element_type | solution.py:84
  36.9 7.7 %all-to-all-done.2 = bf16[128,2,2048]{0,2,1:T(8,128)(2,1)S(1)} async-done(((bf16[128,2,2048]{0,2,1:T(8,128)(2,1)}), bf16[128,2,2048]{0,2,1:T(8,128)(2,1)S(1)}, u32[]{:S(2)}, u32[]{:S(2)}) %all-to-all-start.2) | async-done | bytes 1048608 | tf_op jit(solution)/shard_map/all_to_all | solution.py:154
  46.0 1.6 copy.41
  47.6 4.2 %while.62 = (s32[]{:T(128)}, f32[8,2048]{1,0:T(8,128)S(1)}, f32[8,2048]{1,0:T(8,128)S(1)}, f32[128,2048]{1,0:T(8,128)S(1)}, s32[]{:T(128)}, /*index=5*/s32[]{:T(128)}) while((s32[]{:T(128)}, f32[8,2048]{1,0:T(8,128)S(1)}, f32[8,2048]{1,0:T(8,128)S(1)}, f32[128,2048]{1,0:T(8,128)S(1)}, s32[]{:T(128)}, /*index=5*/s32[]{:T(128)}) %tuple.147), condition=%wide.region_6.7_spmd.clone, body=%wide.region_4.6_spmd.clone.sunk | while | flops 786690 | bytes 1098829 | solution.py:91
  52.1 4.2 %while.63 = (s32[]{:T(128)}, f32[8,2048]{1,0:T(8,128)S(1)}, f32[8,2048]{1,0:T(8,128)S(1)}, f32[128,2048]{1,0:T(8,128)S(1)}, s32[]{:T(128)}, /*index=5*/s32[]{:T(128)}) while((s32[]{:T(128)}, f32[8,2048]{1,0:T(8,128)S(1)}, f32[8,2048]{1,0:T(8,128)S(1)}, f32[128,2048]{1,0:T(8,128)S(1)}, s32[]{:T(128)}, /*index=5*/s32[]{:T(128)}) %tuple.162), condition=%wide.region_9.10_spmd.clone, body=%wide.region_7.9_spmd.clone.sunk | while | flops 786690 | bytes 1098829 | solution.py:91
  62.3 4.4 %all-to-all-start = ((bf16[128,2,2048]{2,0,1:T(8,128)(2,1)}), bf16[128,2,2048]{2,0,1:T(8,128)(2,1)}, u32[]{:S(2)}, u32[]{:S(2)}) async-start(bf16[128,2,2048]{2,0,1:T(8,128)(2,1)} %copy.37), calls=%async_computation | async-start | bytes 2097152 | tf_op jit(solution)/shard_map/all_to_all | solution.py:152
  66.7 31.9 %all-reduce.2 = (f32[16]{0:T(128)S(1)}, f32[16]{0:T(128)S(1)}) all-reduce(f32[16]{0:T(128)S(1)} %dynamic-update-slice, f32[16]{0:T(128)S(1)} %dynamic-update-slice.1), channel_id=1, replica_groups=mesh['ctx'=16,'head'=2] {'ctx'}, use_global_device_ids=true, to_apply=%add | all-reduce | flops 32 | bytes 256
  99.7 67.5 %while.64 = (s32[]{:T(128)}, f32[8,2048]{1,0:T(8,128)S(1)}, s32[]{:T(128)}, f32[16]{0:T(128)S(1)}, f32[16]{0:T(128)S(1)}, /*index=5*/f32[16,8,2048]{2,1,0:T(8,128)}, f32[8,256]{1,0:T(8,128)S(1)}, s32[]{:T(128)}, s32[]{:T(128)}) while((s32[]{:T(128)}, f32[8,2048]{1,0:T(8,128)S(1)}, s32[]{:T(128)}, f32[16]{0:T(128)S(1)}, ...), condition=%wide.region_12.13_spmd.clone, body=%wide.region_11.12_spmd.clone.sunk | while | flops 114692 | bytes 467093 | solution.py:28
  101.8 2.1 fusion.64
  106.0 2.1 fusion.64
  110.2 2.1 fusion.64
  114.4 2.1 fusion.64
  118.6 2.1 fusion.64
  122.8 2.1 fusion.64
  127.1 2.1 fusion.64
  131.3 2.1 fusion.64
  135.5 2.1 fusion.64
  139.7 2.1 fusion.64
  143.9 2.1 fusion.64
  148.2 2.1 fusion.64
  152.4 2.1 fusion.64
  156.6 2.1 fusion.64
  160.8 2.1 fusion.64
  165.0 2.1 fusion.64
  167.2 26.8 %while.66 = (s32[]{:T(128)}, f32[128,2048]{0,1:T(8,128)}, f32[8,2048]{1,0:T(8,128)S(1)}, f32[8,2048]{1,0:T(8,128)S(1)}, f32[128,2048]{0,1:T(8,128)S(1)}, /*index...) while((s32[]{:T(128)}, f32[128,2048]{0,1:T(8,128)}, ...), condition=%wide.region_16.17_spmd.clone.clone, body=%wide.region_15.16_spmd.clone.clone.sunk | while | flops 405084288 | bytes 3246719 | solution.py:77
  167.3 3.0 %fusion.72 = f32[128,2048]{0,1:T(8,128)} fusion(f32[128,2048]{0,1:T(8,128)} %get-tuple-element.959, f32[128,2048]{0,1:T(8,128)S(1)} %get-tuple-element.973, f32[2048]{0:T(1024)S(1)} %bitcast.126, f32[128]{0:T(128)} %get-tuple-element.974, f32[2048]{0:T(1024)S(1)} %bitcast.118, f32[128]{0:T(128)S(1)} %iota_convert_fusion.6, f32[2048]{0:T(1024)S(1)} %bitcast.120, ...), kind=kOutput, calls=%fused_computation.43.clone.1 | convolution fusion | flops 405078016 | bytes 3180545 | tf_op jit(solution)/shard_map/while/body/eval_jaxpr/dot_general | solution.py:69
  170.4 3.3 %fusion.72 = f32[128,2048]{0,1:T(8,128)} fusion(f32[128,2048]{0,1:T(8,128)} %get-tuple-element.959, f32[128,2048]{0,1:T(8,128)S(1)} %get-tuple-element.973, f32[2048]{0:T(1024)S(1)} %bitcast.126, f32[128]{0:T(128)} %get-tuple-element.974, f32[2048]{0:T(1024)S(1)} %bitcast.118, f32[128]{0:T(128)S(1)} %iota_convert_fusion.6, f32[2048]{0:T(1024)S(1)} %bitcast.120, ...), kind=kOutput, calls=%fused_computation.43.clone.1 | convolution fusion | flops 405078016 | bytes 3180545 | tf_op jit(solution)/shard_map/while/body/eval_jaxpr/dot_general | solution.py:69
  173.8 3.3 %fusion.72 = f32[128,2048]{0,1:T(8,128)} fusion(f32[128,2048]{0,1:T(8,128)} %get-tuple-element.959, f32[128,2048]{0,1:T(8,128)S(1)} %get-tuple-element.973, f32[2048]{0:T(1024)S(1)} %bitcast.126, f32[128]{0:T(128)} %get-tuple-element.974, f32[2048]{0:T(1024)S(1)} %bitcast.118, f32[128]{0:T(128)S(1)} %iota_convert_fusion.6, f32[2048]{0:T(1024)S(1)} %bitcast.120, ...), kind=kOutput, calls=%fused_computation.43.clone.1 | convolution fusion | flops 405078016 | bytes 3180545 | tf_op jit(solution)/shard_map/while/body/eval_jaxpr/dot_general | solution.py:69
  177.2 3.3 %fusion.72 = f32[128,2048]{0,1:T(8,128)} fusion(f32[128,2048]{0,1:T(8,128)} %get-tuple-element.959, f32[128,2048]{0,1:T(8,128)S(1)} %get-tuple-element.973, f32[2048]{0:T(1024)S(1)} %bitcast.126, f32[128]{0:T(128)} %get-tuple-element.974, f32[2048]{0:T(1024)S(1)} %bitcast.118, f32[128]{0:T(128)S(1)} %iota_convert_fusion.6, f32[2048]{0:T(1024)S(1)} %bitcast.120, ...), kind=kOutput, calls=%fused_computation.43.clone.1 | convolution fusion | flops 405078016 | bytes 3180545 | tf_op jit(solution)/shard_map/while/body/eval_jaxpr/dot_general | solution.py:69
  180.6 3.3 %fusion.72 = f32[128,2048]{0,1:T(8,128)} fusion(f32[128,2048]{0,1:T(8,128)} %get-tuple-element.959, f32[128,2048]{0,1:T(8,128)S(1)} %get-tuple-element.973, f32[2048]{0:T(1024)S(1)} %bitcast.126, f32[128]{0:T(128)} %get-tuple-element.974, f32[2048]{0:T(1024)S(1)} %bitcast.118, f32[128]{0:T(128)S(1)} %iota_convert_fusion.6, f32[2048]{0:T(1024)S(1)} %bitcast.120, ...), kind=kOutput, calls=%fused_computation.43.clone.1 | convolution fusion | flops 405078016 | bytes 3180545 | tf_op jit(solution)/shard_map/while/body/eval_jaxpr/dot_general | solution.py:69
  183.9 3.3 %fusion.72 = f32[128,2048]{0,1:T(8,128)} fusion(f32[128,2048]{0,1:T(8,128)} %get-tuple-element.959, f32[128,2048]{0,1:T(8,128)S(1)} %get-tuple-element.973, f32[2048]{0:T(1024)S(1)} %bitcast.126, f32[128]{0:T(128)} %get-tuple-element.974, f32[2048]{0:T(1024)S(1)} %bitcast.118, f32[128]{0:T(128)S(1)} %iota_convert_fusion.6, f32[2048]{0:T(1024)S(1)} %bitcast.120, ...), kind=kOutput, calls=%fused_computation.43.clone.1 | convolution fusion | flops 405078016 | bytes 3180545 | tf_op jit(solution)/shard_map/while/body/eval_jaxpr/dot_general | solution.py:69
  187.3 3.3 %fusion.72 = f32[128,2048]{0,1:T(8,128)} fusion(f32[128,2048]{0,1:T(8,128)} %get-tuple-element.959, f32[128,2048]{0,1:T(8,128)S(1)} %get-tuple-element.973, f32[2048]{0:T(1024)S(1)} %bitcast.126, f32[128]{0:T(128)} %get-tuple-element.974, f32[2048]{0:T(1024)S(1)} %bitcast.118, f32[128]{0:T(128)S(1)} %iota_convert_fusion.6, f32[2048]{0:T(1024)S(1)} %bitcast.120, ...), kind=kOutput, calls=%fused_computation.43.clone.1 | convolution fusion | flops 405078016 | bytes 3180545 | tf_op jit(solution)/shard_map/while/body/eval_jaxpr/dot_general | solution.py:69
  190.7 3.3 %fusion.72 = f32[128,2048]{0,1:T(8,128)} fusion(f32[128,2048]{0,1:T(8,128)} %get-tuple-element.959, f32[128,2048]{0,1:T(8,128)S(1)} %get-tuple-element.973, f32[2048]{0:T(1024)S(1)} %bitcast.126, f32[128]{0:T(128)} %get-tuple-element.974, f32[2048]{0:T(1024)S(1)} %bitcast.118, f32[128]{0:T(128)S(1)} %iota_convert_fusion.6, f32[2048]{0:T(1024)S(1)} %bitcast.120, ...), kind=kOutput, calls=%fused_computation.43.clone.1 | convolution fusion | flops 405078016 | bytes 3180545 | tf_op jit(solution)/shard_map/while/body/eval_jaxpr/dot_general | solution.py:69
  194.1 14.2 %while.65 = (s32[]{:T(128)}, f32[128,2048]{0,1:T(8,128)S(1)}, f32[8,2048]{1,0:T(8,128)S(1)}, f32[8,2048]{1,0:T(8,128)S(1)}, f32[128,2048]{0,1:T(8,128)S(1)}, /*i...) while((s32[]{:T(128)}, f32[128,2048]{0,1:T(8,128)S(1)}, ...), condition=%wide.region_14.15_spmd.clone.clone, body=%wide.region_13.14_spmd.clone.clone.sunk | while | flops 405084288 | bytes 3246719 | solution.py:77
  194.1 1.7 fusion.68
  195.9 1.7 fusion.68
  197.7 1.7 fusion.68
  199.5 1.7 fusion.68
  201.3 1.7 fusion.68
  203.0 1.7 fusion.68
  204.8 1.7 fusion.68
  206.6 1.7 fusion.68
  208.3 1.5 add_convert_fusion.1
  212.0 14.6 %all_to_all.58 = bf16[2,128,2048]{2,1,0:T(8,128)(2,1)S(1)} all-to-all(bf16[2,128,2048]{2,1,0:T(8,128)(2,1)S(1)} %bitcast_multiply_fusion), channel_id=1, replica_groups=mesh['ctx'=16,'head'=2] {'head'}, dimensions={0} | all-to-all | bytes 2097152 | tf_op jit(solution)/shard_map/all_to_all | solution.py:160
  (243 shorter events, 57.3 us)
Async XLA Ops:
  8.8 4.4 %copy-start.9 = (s32[16]{0:T(128)S(1)}, s32[16]{0:T(128)}, u32[]{:S(2)}) copy-start(s32[16]{0:T(128)} %param.23) | copy-start | bytes 196
  8.8 6.6 %copy-start.3 = (bf16[128,4096]{1,0:T(8,128)(2,1)S(1)}, bf16[128,4096]{1,0:T(8,128)(2,1)}, u32[]{:S(2)}) copy-start(bf16[128,4096]{1,0:T(8,128)(2,1)} %param.19) | copy-start | bytes 3145732
  8.8 18.8 %all-to-all-start.1 = ((bf16[128,2,2048]{0,2,1:T(8,128)(2,1)}), bf16[128,2,2048]{0,2,1:T(8,128)(2,1)S(1)}, u32[]{:S(2)}, u32[]{:S(2)}) async-start(bf16[128,2,2048]{0,2,1:T(8,128)(2,1)} %bitcast.4), calls=%async_computation.1 | async-start | bytes 2097152 | tf_op jit(solution)/shard_map/all_to_all | solution.py:153
  14.1 19.5 %copy-start.5 = (s32[128]{0:T(128)}, s32[128]{0:T(128)S(1)}, u32[]{:S(2)}) copy-start(s32[128]{0:T(128)S(1)} %get-tuple-element.954) | copy-start | bytes 1540
  27.6 3.8 %copy-start.7 = (f32[512,8]{0,1:T(8,128)S(1)}, f32[512,8]{0,1:T(8,128)}, u32[]{:S(2)}) copy-start(f32[512,8]{0,1:T(8,128)} %param.20) | copy-start | bytes 49156
  27.6 3.8 %copy-start.8 = (f32[512,8]{0,1:T(8,128)S(1)}, f32[512,8]{0,1:T(8,128)}, u32[]{:S(2)}) copy-start(f32[512,8]{0,1:T(8,128)} %param.21) | copy-start | bytes 49156
  27.6 17.0 %all-to-all-start.2 = ((bf16[128,2,2048]{0,2,1:T(8,128)(2,1)}), bf16[128,2,2048]{0,2,1:T(8,128)(2,1)S(1)}, u32[]{:S(2)}, u32[]{:S(2)}) async-start(bf16[128,2,2048]{0,2,1:T(8,128)(2,1)} %bitcast.5), calls=%async_computation.2 | async-start | bytes 2097152 | tf_op jit(solution)/shard_map/all_to_all | solution.py:154
  31.3 68.3 %all-gather.3.cloned.1.call-start = ((), (), s32[]{:S(2)}) async-start(), calls=%async_computation.4 | async-start | bytes 1114112 | tf_op jit(solution)/shard_map/all_gather | solution.py:16
  44.7 54.8 %copy-start.2 = (bf16[2,128,2048]{1,2,0:T(8,128)(2,1)}, bf16[2,128,2048]{1,2,0:T(8,128)(2,1)S(1)}, u32[]{:S(2)}) copy-start(bf16[2,128,2048]{1,2,0:T(8,128)(2,1)S(1)} %multiply_bitcast_fusion) | copy-start | bytes 3145732
  52.1 6.3 %copy-start.4 = (bf16[128,4096]{1,0:T(8,128)(2,1)S(1)}, bf16[128,4096]{1,0:T(8,128)(2,1)}, u32[]{:S(2)}) copy-start(bf16[128,4096]{1,0:T(8,128)(2,1)} %param.17) | copy-start | bytes 3145732
  59.1 1.3 copy-start.10
  62.3 148.3 %all-to-all-start = ((bf16[128,2,2048]{2,0,1:T(8,128)(2,1)}), bf16[128,2,2048]{2,0,1:T(8,128)(2,1)}, u32[]{:S(2)}, u32[]{:S(2)}) async-start(bf16[128,2,2048]{2,0,1:T(8,128)(2,1)} %copy.37), calls=%async_computation | async-start | bytes 2097152 | tf_op jit(solution)/shard_map/all_to_all | solution.py:152
  167.2 26.8 %copy-start = (f32[128,2048]{0,1:T(8,128)S(1)}, f32[128,2048]{0,1:T(8,128)}, u32[]{:S(2)}) copy-start(f32[128,2048]{0,1:T(8,128)} %custom-call.1) | copy-start | bytes 3145732
  167.2 26.8 %copy-start.6 = (f32[128]{0:T(128)S(1)}, f32[128]{0:T(128)}, u32[]{:S(2)}) copy-start(f32[128]{0:T(128)} %get-tuple-element.919) | copy-start | bytes 1540
  194.0 14.2 %copy-start.1 = (f32[128,2048]{0,1:T(8,128)S(1)}, f32[128,2048]{0,1:T(8,128)}, u32[]{:S(2)}) copy-start(f32[128,2048]{0,1:T(8,128)} %get-tuple-element.333) | copy-start | bytes 3145732
  194.0 14.2 %dynamic-slice-start = ((f32[4096]{0:T(1024)}, s32[]{:T(128)}), f32[2048]{0:T(1024)S(1)}, s32[]{:S(2)}) async-start(f32[4096]{0:T(1024)} %param.22, s32[]{:T(128)} %select_n.37), calls=%async_computation.5 | async-start | bytes 16896 | tf_op jit(solution)/shard_map/dynamic_slice | solution.py:147
Sparse Core Ops, SparseCore 0:
  57.1 38.1 all-gather.2
where the time goes:
time: 237 us; the launch traced here: 235 us
  local copies, waits for them, and re-layouts  51.2 us (22%)
  other arithmetic  48.8 us (21%)
  blocking collectives  46.5 us (20%)
  matrix products  39.6 us (17%)
  waiting for transfers between devices  18.6 us (8%)
  between operations  16.4 us (7%)
  starting transfers between devices  12.5 us (5%)
    dot_general x16, matrix products, per_mode(): jnp.dot(mask_matrix, scaled, precision=highest, preferred_element_type=jn...  39.6 us
    select_n x16, other arithmetic, hop(): return jax.tree.map(lambda a, b: jnp.where(reached, a, b), new, before)  34.2 us
    unnamed x1, blocking collectives  31.9 us
    dynamic_slice x32, local copies, waits for them, and re-layouts, hop(): new = combine(before, jax.tree.map(lambda part: part[k], everything))  19.4 us
    all_to_all x1, blocking collectives, shards(): lax.all_to_all(query_part * smoothed, 'head', split_axis=0, concat_axis=1...  14.6 us
    all_to_all x1, waiting for transfers between devices, shards(): lax.all_to_all(key_gate, 'head', split_axis=1, concat_axis=0, tiled=True)  10.9 us
    reshape x18, local copies, waits for them, and re-layouts, widen(): return jnp.repeat(table.T, group_width, axis=1)  9.35 us
    unnamed x32, local copies, waits for them, and re-layouts  8.03 us
  transfers between devices with their start and end apart: 4, of which 2 were waited for; matrix products, arithmetic and copies ran while one was open for 52% of the time, Pallas kernels for 0%

commit v1 on v0

v1 whole, which is shorter than its diff:
```python
import functools
import math

import jax
import jax.numpy as jnp
from jax import lax
from jax.experimental import pallas as pl
from jax.experimental.pallas import tpu as pltpu
from jax.sharding import PartitionSpec as P

LANES = 128
MESH = pl.DeviceIdType.MESH
f32 = jnp.float32
bf16 = jnp.bfloat16


def doc_start(tokens, ends):
    start = jnp.zeros_like(tokens)
    for end in ends:
        start = jnp.maximum(start, jnp.where(tokens >= end, end, 0))
    return start


def kernel(cfg, lengths, q_hbm, k_hbm, v_hbm, rate_rows, weight_rows, chan_rate, chan_weight, skip,
           out_hbm, q_buf, k_buf, v_buf, out_buf, mixed, inner, cross_table,
           state_buf, gather_buf, prefix_buf, reply_buf, enter_buf, exit_buf, far_buf,
           load_sem, store_sem, send1, recv1, send2, recv2, send3, recv3):
    ctx_count, head_count, block, reach = cfg
    devices = ctx_count * head_count
    tok, chans = mixed.shape
    modes = chan_rate.shape[0]
    lane_blocks = chans // LANES
    per_slice = lane_blocks // block
    group_width = LANES * modes // LANES
    block_count = devices // block
    me = lax.axis_index("ctx") * head_count + lax.axis_index("head")
    zone, pos = me // block, me % block
    span = me * tok

    def where_is(index):
        return (index // head_count, index % head_count)

    loads = []
    for n, (src, dst) in enumerate(((k_hbm, k_buf), (v_hbm, v_buf), (q_hbm, q_buf))):
        loads.append(pltpu.make_async_copy(src, dst, load_sem.at[n]))
        loads[-1].start()

    barrier = pltpu.get_barrier_semaphore()
    mates = [zone * block + (pos + s) % block for s in range(1, block)]
    for mate in mates:
        pl.semaphore_signal(barrier, inc=1, device_id=where_is(mate), device_id_type=MESH)
    for k in range(1, reach + 1):
        @pl.when(zone + k < block_count)
        def _(k=k):
            pl.semaphore_signal(barrier, inc=1, device_id=where_is(me + k * block), device_id_type=MESH)

        @pl.when(zone >= k)
        def _(k=k):
            pl.semaphore_signal(barrier, inc=1, device_id=where_is(me - k * block), device_id_type=MESH)

    ends, total = [], jnp.int32(0)
    for n in range(lengths.shape[0]):
        total = total + lengths[n]
        ends.append(total)

    def start_of(token):
        return doc_start(jnp.full((1, LANES), token, jnp.int32), ends)

    rows = lax.broadcasted_iota(jnp.int32, (tok, LANES), 0)
    gr = lax.broadcasted_iota(jnp.int32, (LANES, LANES), 0) // modes
    gc = lax.broadcasted_iota(jnp.int32, (LANES, LANES), 1) // group_width
    diagonal = gr == gc

    tail_start = start_of(span + tok - 1) - span
    tail = rows >= tail_start
    left = (tok - 1 - rows).astype(f32)

    loads[0].wait()
    loads[1].wait()

    def local(b, _):
        cols = pl.ds(pl.multiple_of(b * LANES, LANES), LANES)
        x = k_buf[:, cols] * v_buf[:, cols]
        mixed[:, cols] = x
        rate = rate_rows[pl.ds(b, 1), :]
        table = jnp.where(tail, jnp.exp(-rate * left), 0.0).astype(bf16)
        full = lax.dot_general(table, x, (((0,), (0,)), ((), ())), preferred_element_type=f32)
        full = jnp.where(diagonal, full, 0.0)
        state = jnp.sum(full.reshape(LANES // modes, modes, LANES), axis=0)
        state_buf[b // per_slice, :, pl.ds(pl.multiple_of((b % per_slice) * LANES, LANES), LANES)] = state.astype(state_buf.dtype)
        return 0

    lax.fori_loop(0, lane_blocks, local, 0, unroll=4)

    expected = (block - 1)
    for k in range(1, reach + 1):
        expected = expected + jnp.where(zone + k < block_count, 1, 0) + jnp.where(zone >= k, 1, 0)
    pl.semaphore_wait(barrier, expected)

    first = []
    for s, mate in enumerate(mates):
        first.append(pltpu.make_async_remote_copy(
            src_ref=state_buf.at[(pos + s + 1) % block], dst_ref=gather_buf.at[pos],
            send_sem=send1.at[s], recv_sem=recv1.at[s],
            device_id=where_is(mate), device_id_type=MESH))
        first[-1].start()
    gather_buf[pos] = state_buf[pos]

    row_tok = span + rows
    row_start = doc_start(row_tok, ends) - span
    lane_iota = lax.broadcasted_iota(jnp.int32, (tok, tok), 1)
    row_iota = lax.broadcasted_iota(jnp.int32, (tok, tok), 0)
    mask = jnp.where((lane_iota >= row_start[:, :1]) & (lane_iota <= row_iota), 1.0, 0.0).astype(bf16)
    linked = row_start < 0
    ahead = (rows + 1).astype(f32)

    wide = 2 * LANES
    wide_blocks = chans // wide
    eights = lax.broadcasted_iota(jnp.int32, (8, wide), 0).astype(f32)

    def conv(b, _):
        cols = pl.ds(pl.multiple_of(b * wide, wide), wide)
        x = mixed[:, cols].astype(f32)
        total = skip[:, cols] * x
        for r in range(modes):
            rate = chan_rate[r:r + 1, cols]
            up = jnp.exp(rate * eights)
            down = chan_weight[r:r + 1, cols] * jnp.exp(-rate * eights)
            up_step = jnp.broadcast_to(jnp.exp(8.0 * rate), up.shape)
            down_step = jnp.broadcast_to(jnp.exp(-8.0 * rate), up.shape)
            ups, downs = [], []
            for _p in range(tok // 8):
                ups.append(up)
                downs.append(down)
                up, down = up * up_step, down * down_step
            scaled = (x * jnp.concatenate(ups, axis=0)).astype(bf16)
            summed = jnp.dot(mask, scaled, preferred_element_type=f32)
            total = total + jnp.concatenate(downs, axis=0) * summed
        inner[:, cols] = total
        return 0

    def entering_table(b, _):
        cols = pl.ds(pl.multiple_of(b * LANES, LANES), LANES)
        rate = rate_rows[pl.ds(b, 1), :]
        weight = weight_rows[pl.ds(b, 1), :]
        cross_table[:, cols] = jnp.where(linked, weight * jnp.exp(-rate * ahead), 0.0).astype(bf16)
        return 0

    half = wide_blocks // 2
    lax.fori_loop(0, half, conv, 0)

    width = chans // block
    slice_rate = chan_rate[:, pl.ds(pl.multiple_of(pos * width, width), width)]
    decay = jnp.exp(-slice_rate * float(tok))

    def keep_of(index):
        crossing = start_of(index * tok + tok - 1) < index * tok
        return jnp.where(crossing, 1.0, 0.0)[:, :1]

    for copy in first:
        copy.wait()
    carry = jnp.zeros(slice_rate.shape, f32)
    factor = jnp.ones(slice_rate.shape, f32)
    factors = []
    for e in range(block):
        prefix_buf[e] = carry
        factors.append(factor)
        step = keep_of(zone * block + e) * decay
        carry = step * carry + gather_buf[e].astype(f32)
        factor = step * factor
    exit_buf[...] = carry.astype(exit_buf.dtype)

    def onward(k):
        return pltpu.make_async_remote_copy(
            src_ref=exit_buf, dst_ref=far_buf.at[k - 1],
            send_sem=send2.at[k - 1], recv_sem=recv2.at[k - 1],
            device_id=where_is(me + k * block), device_id_type=MESH)

    for k in range(1, reach + 1):
        @pl.when(zone + k < block_count)
        def _(k=k):
            onward(k).start()

    lax.fori_loop(0, lane_blocks, entering_table, 0, unroll=4)

    for k in range(1, reach + 1):
        @pl.when(zone >= k)
        def _(k=k):
            onward(k).wait_recv()

        @pl.when(zone < k)
        def _(k=k):
            far_buf[k - 1] = jnp.zeros(far_buf.shape[1:], far_buf.dtype)

    last_start = start_of(jnp.maximum(zone * block * tok - 1, 0))
    far = jnp.zeros(slice_rate.shape, f32)
    for k in range(1, reach + 1):
        same = (last_start < (zone - k + 1) * block * tok)
        flag = jnp.where(same, 1.0, 0.0)[:, :1]
        scale = flag * jnp.exp(-slice_rate * float(tok * block * (k - 1)))
        far = far + scale * far_buf[k - 1].astype(f32)
    for e in range(block):
        reply_buf[e] = (prefix_buf[e] + factors[e] * far).astype(reply_buf.dtype)

    last = []
    for s, mate in enumerate(mates):
        last.append(pltpu.make_async_remote_copy(
            src_ref=reply_buf.at[(pos + s + 1) % block], dst_ref=enter_buf.at[pos],
            send_sem=send3.at[s], recv_sem=recv3.at[s],
            device_id=where_is(mate), device_id_type=MESH))
        last[-1].start()
    enter_buf[pos] = reply_buf[pos]

    lax.fori_loop(half, wide_blocks, conv, 0)
    loads[2].wait()
    for copy in last:
        copy.wait()

    def finish(b, _):
        cols = pl.ds(pl.multiple_of(b * LANES, LANES), LANES)
        state = enter_buf[b // per_slice, :, pl.ds(pl.multiple_of((b % per_slice) * LANES, LANES), LANES)].astype(f32)
        spread = jnp.where(diagonal, jnp.concatenate([state] * (LANES // modes), axis=0), 0.0).astype(bf16)
        cross = jnp.dot(cross_table[:, cols], spread, preferred_element_type=f32)
        smoothed = (inner[:, cols] + cross).astype(bf16)
        out_buf[:, cols] = q_buf[:, cols] * smoothed
        return 0

    lax.fori_loop(0, lane_blocks, finish, 0, unroll=4)
    store = pltpu.make_async_copy(out_buf, out_hbm, store_sem)
    store.start()
    for k in range(1, reach + 1):
        @pl.when(zone + k < block_count)
        def _(k=k):
            onward(k).wait_send()
    store.wait()


def shards(query_gate, key_gate, values, rate_mix, residue, skip_gain, doc_lengths):
    ctx_count = lax.axis_size("ctx")
    head_count = lax.axis_size("head")
    devices = ctx_count * head_count
    tok, chans = query_gate.shape
    groups, modes = rate_mix.shape
    group_width = chans // groups
    total_tokens = tok * devices
    longest = total_tokens // 4
    block = min(devices // 4, chans // (4 * LANES))
    reach = -(-longest // (tok * block))
    rate = jnp.exp(-math.log(30.0) - rate_mix * math.log(float(total_tokens)))
    weight = residue * jnp.sqrt(-jnp.expm1(-2.0 * rate))
    rate_rows = rate.reshape(-1, LANES)
    weight_rows = weight.reshape(-1, LANES)
    rate_chan = jnp.repeat(rate.T, group_width, axis=1)
    weight_chan = jnp.repeat(weight.T, group_width, axis=1)
    width = chans // block
    wire = bf16
    vmem = pl.BlockSpec(memory_space=pltpu.VMEM)
    anywhere = pl.BlockSpec(memory_space=pl.ANY)
    dma = pltpu.SemaphoreType.DMA
    return pl.pallas_call(
        functools.partial(kernel, (ctx_count, head_count, block, reach)),
        out_shape=jax.ShapeDtypeStruct((tok, chans), bf16),
        in_specs=[pl.BlockSpec(memory_space=pltpu.SMEM), anywhere, anywhere, anywhere] + [vmem] * 5,
        out_specs=anywhere,
        scratch_shapes=[
            pltpu.VMEM((tok, chans), bf16), pltpu.VMEM((tok, chans), bf16),
            pltpu.VMEM((tok, chans), bf16), pltpu.VMEM((tok, chans), bf16),
            pltpu.VMEM((tok, chans), bf16), pltpu.VMEM((tok, chans), f32),
            pltpu.VMEM((tok, chans), bf16),
            pltpu.VMEM((block, modes, width), wire),
            pltpu.VMEM((block, modes, width), wire),
            pltpu.VMEM((block, modes, width), f32),
            pltpu.VMEM((block, modes, width), wire),
            pltpu.VMEM((block, modes, width), wire),
            pltpu.VMEM((modes, width), wire),
            pltpu.VMEM((reach, modes, width), wire),
            dma((3,)), dma, dma((block - 1,)), dma((block - 1,)),
            dma((reach,)), dma((reach,)), dma((block - 1,)), dma((block - 1,)),
        ],
        compiler_params=pltpu.CompilerParams(collective_id=0, has_side_effects=True,
                                             vmem_limit_bytes=32 * 1024 * 1024),
    )(doc_lengths, query_gate, key_gate, values, rate_rows, weight_rows, rate_chan, weight_chan, skip_gain.reshape(1, -1))


def solution(mesh):
    spans = P(("ctx", "head"), None)
    return jax.shard_map(
        shards,
        mesh=mesh,
        in_specs=(spans, spans, spans, P(), P(), P(), P()),
        out_specs=spans,
        check_vma=False,
    )
```

time: 237 us -> 23.8 us (0.10)
  the two profiles are of different devices: /device:TPU:0 before, /device:TPU:25 now
where the time goes in v1:
time: 23.8 us; the launch traced here: 23.5 us
  Pallas kernels  14.5 us (61%)
  local copies, waits for them, and re-layouts  8.07 us (34%)
  other arithmetic  0.76 us (3%)
    pallas_call x1, Pallas kernels, shards(): pl.pallas_call(functools.partial(kernel, (ctx_count, head_count, block, r...  14.5 us
    reshape x1, local copies, waits for them, and re-layouts, shards(): weight_chan = jnp.repeat(weight.T, group_width, axis=1)  2.78 us
    broadcast_in_dim x1, local copies, waits for them, and re-layouts, shards(): weight_chan = jnp.repeat(weight.T, group_width, axis=1)  1.95 us
    reshape x1, local copies, waits for them, and re-layouts, shards(): rate_chan = jnp.repeat(rate.T, group_width, axis=1)  1.2 us
    unnamed x11, local copies, waits for them, and re-layouts  1 us
    transpose x1, other arithmetic, shards(): rate_chan = jnp.repeat(rate.T, group_width, axis=1)  0.76 us
    broadcast_in_dim x1, local copies, waits for them, and re-layouts, shards(): rate_chan = jnp.repeat(rate.T, group_width, axis=1)  0.6 us

profile of v1, /device:TPU:25, one launch (start us, length us, event | category | flops | bytes accessed | tf_op | source)
XLA Modules:
  0.0 23.5 jit_solution(384592896061260525)
XLA Ops:
  0.0 0.8 %fusion = (f32[8,512]{1,0:T(8,128)S(1)}, f32[512,8]{0,1:T(8,128)S(1)}, f32[512,8]{0,1:T(8,128)S(1)}) fusion(f32[512,8]{0,1:T(8,128)} %param.10, f32[512,8]{0,1:T(8,128)} %param.11), kind=kLoop, calls=%fused_computation.2 | loop fusion | flops 20480 | bytes 81920 | tf_op jit(solution)/shard_map/transpose | solution.py:253
  0.8 0.1 copy.10
  0.9 0.2 reshape.15.rate_rows
  1.1 0.1 copy.11
  1.2 0.2 reshape.16.weight_rows
  1.3 0.6 %broadcast_in_dim.6 = f32[8,512,8]{2,1,0:T(8,128)S(1)} broadcast(f32[8,512]{1,0:T(8,128)S(1)} %get-tuple-element.5), dimensions={0,1} | broadcast | bytes 147456 | tf_op jit(solution)/shard_map/broadcast_in_dim | solution.py:253
  1.9 1.2 %reshape.17.chan_rate = f32[8,4096]{1,0:T(8,128)S(1)} reshape(f32[8,512,8]{2,1,0:T(8,128)S(1)} %broadcast_in_dim.6) | data formatting | bytes 262144 | tf_op jit(solution)/shard_map/reshape | solution.py:253
  3.1 0.0 copy-start
  3.1 0.0 copy-start.1
  3.1 0.0 copy-start.2
  3.2 0.0 copy-start.3
  3.2 0.0 copy-start.4
  3.2 1.9 %broadcast_in_dim.7 = f32[8,512,8]{2,1,0:T(8,128)} broadcast(f32[8,512]{1,0:T(8,128)S(1)} %bitcast.5), dimensions={0,1} | broadcast | bytes 147456 | tf_op jit(solution)/shard_map/broadcast_in_dim | solution.py:254
  5.1 2.8 %reshape.18.chan_weight = f32[8,4096]{1,0:T(8,128)S(1)} reshape(f32[8,512,8]{2,1,0:T(8,128)} %broadcast_in_dim.7) | data formatting | bytes 262144 | tf_op jit(solution)/shard_map/reshape | solution.py:254
  7.9 0.0 copy-done
  7.9 0.0 copy-done.1
  7.9 0.0 copy-done.2
  7.9 0.0 copy-done.3
  7.9 0.0 copy-done.4
  8.0 14.5 %shard_map.73 = bf16[128,4096]{1,0:T(8,128)(2,1)S(1)} custom-call(s32[16]{0:T(128)S(1)} %copy-done.4, bf16[128,4096]{1,0:T(8,128)(2,1)S(1)} %copy-done, bf16[128,4096]{1,0:T(8,128)(2,1)S(1)} %copy-done.1, bf16[128,4096]{1,0:T(8,128)(2,1)S(1)} %copy-done.2, f32[32,128]{1,0:T(8,128)S(1)} %reshape.15.rate_rows, f32[32,128]{1,0:T(8,128)S(1)} %reshape.16.weight_rows, ...), custom_call_target="tpu_custom_call" | custom-call | tf_op jit(solution)/shard_map/pallas_call | solution.py:260
  22.5 1.0 %copy.13 = bf16[128,4096]{1,0:T(8,128)(2,1)} copy(bf16[128,4096]{1,0:T(8,128)(2,1)S(1)} %shard_map.73) | data formatting | bytes 2097152
Async XLA Ops:
  3.1 4.8 %copy-start = (bf16[128,4096]{1,0:T(8,128)(2,1)S(1)}, bf16[128,4096]{1,0:T(8,128)(2,1)}, u32[]{:S(2)}) copy-start(bf16[128,4096]{1,0:T(8,128)(2,1)} %q_hbm.1) | copy-start | bytes 3145732
  3.1 4.8 %copy-start.1 = (bf16[128,4096]{1,0:T(8,128)(2,1)S(1)}, bf16[128,4096]{1,0:T(8,128)(2,1)}, u32[]{:S(2)}) copy-start(bf16[128,4096]{1,0:T(8,128)(2,1)} %k_hbm.1) | copy-start | bytes 3145732
  3.1 4.8 %copy-start.2 = (bf16[128,4096]{1,0:T(8,128)(2,1)S(1)}, bf16[128,4096]{1,0:T(8,128)(2,1)}, u32[]{:S(2)}) copy-start(bf16[128,4096]{1,0:T(8,128)(2,1)} %v_hbm.1) | copy-start | bytes 3145732
  3.2 4.8 %copy-start.3 = (f32[4096]{0:T(1024)S(1)}, f32[4096]{0:T(1024)}, u32[]{:S(2)}) copy-start(f32[4096]{0:T(1024)} %param.12) | copy-start | bytes 49156
  3.2 4.8 %copy-start.4 = (s32[16]{0:T(128)S(1)}, s32[16]{0:T(128)}, u32[]{:S(2)}) copy-start(s32[16]{0:T(128)} %lengths.1) | copy-start | bytes 196

commit v2 on v1

--- a/solution.py
+++ b/solution.py
@@ -21,8 +21,17 @@
     return start
 
 
-def kernel(cfg, lengths, q_hbm, k_hbm, v_hbm, rate_rows, weight_rows, chan_rate, chan_weight, skip,
+def split_three(x):
+    high = x.astype(bf16)
+    rest = x - high.astype(f32)
+    middle = rest.astype(bf16)
+    low = (rest - middle.astype(f32)).astype(bf16)
+    return [high, middle, low]
+
+
+def kernel(cfg, lengths, q_hbm, k_hbm, v_hbm, rate_mix, residue, skip,
            out_hbm, q_buf, k_buf, v_buf, out_buf, mixed, inner, cross_table,
+           chan_rate, chan_weight, rate_row, weight_row,
            state_buf, gather_buf, prefix_buf, reply_buf, enter_buf, exit_buf, far_buf,
            load_sem, store_sem, send1, recv1, send2, recv2, send3, recv3):
     ctx_count, head_count, block, reach = cfg
@@ -71,6 +80,27 @@
     gc = lax.broadcasted_iota(jnp.int32, (LANES, LANES), 1) // group_width
     diagonal = gr == gc
 
+    rate = jnp.exp(-math.log(30.0) - rate_mix[...] * math.log(float(devices * tok)))
+    double = 2.0 * rate
+    one_minus = jnp.where(double < 1e-2,
+                          double * (1.0 - double * (0.5 - double * (1.0 / 6.0 - double / 24.0))),
+                          1.0 - jnp.exp(-double))
+    weight = residue[...] * jnp.sqrt(one_minus)
+    stacked = jnp.concatenate([p.astype(f32) for p in split_three(rate) + split_three(weight)], axis=0).astype(bf16)
+    spread_to = LANES * group_width
+    onto = jnp.where(lax.broadcasted_iota(jnp.int32, (LANES, spread_to), 0)
+                     == lax.broadcasted_iota(jnp.int32, (LANES, spread_to), 1) // group_width, 1.0, 0.0).astype(bf16)
+    own = (lax.broadcasted_iota(jnp.int32, (modes, spread_to), 0)
+           == lax.broadcasted_iota(jnp.int32, (modes, spread_to), 1) % modes)
+    for n in range(rate.shape[1] // LANES):
+        wide_table = jnp.dot(stacked[:, n * LANES:(n + 1) * LANES], onto, preferred_element_type=f32)
+        parts = [wide_table[m * modes:(m + 1) * modes] for m in range(6)]
+        cols = slice(n * spread_to, (n + 1) * spread_to)
+        for m, (table, row) in enumerate(((chan_rate, rate_row), (chan_weight, weight_row))):
+            value = parts[3 * m] + (parts[3 * m + 1] + parts[3 * m + 2])
+            table[:, cols] = value
+            row[:, cols] = jnp.sum(jnp.where(own, value, 0.0), axis=0, keepdims=True)
+
     tail_start = start_of(span + tok - 1) - span
     tail = rows >= tail_start
     left = (tok - 1 - rows).astype(f32)
@@ -82,7 +112,7 @@
         cols = pl.ds(pl.multiple_of(b * LANES, LANES), LANES)
         x = k_buf[:, cols] * v_buf[:, cols]
         mixed[:, cols] = x
-        rate = rate_rows[pl.ds(b, 1), :]
+        rate = rate_row[:, cols]
         table = jnp.where(tail, jnp.exp(-rate * left), 0.0).astype(bf16)
         full = lax.dot_general(table, x, (((0,), (0,)), ((), ())), preferred_element_type=f32)
         full = jnp.where(diagonal, full, 0.0)
@@ -141,8 +171,8 @@
 
     def entering_table(b, _):
         cols = pl.ds(pl.multiple_of(b * LANES, LANES), LANES)
-        rate = rate_rows[pl.ds(b, 1), :]
-        weight = weight_rows[pl.ds(b, 1), :]
+        rate = rate_row[:, cols]
+        weight = weight_row[:, cols]
         cross_table[:, cols] = jnp.where(linked, weight * jnp.exp(-rate * ahead), 0.0).astype(bf16)
         return 0
 
@@ -246,27 +276,23 @@
     longest = total_tokens // 4
     block = min(devices // 4, chans // (4 * LANES))
     reach = -(-longest // (tok * block))
-    rate = jnp.exp(-math.log(30.0) - rate_mix * math.log(float(total_tokens)))
-    weight = residue * jnp.sqrt(-jnp.expm1(-2.0 * rate))
-    rate_rows = rate.reshape(-1, LANES)
-    weight_rows = weight.reshape(-1, LANES)
-    rate_chan = jnp.repeat(rate.T, group_width, axis=1)
-    weight_chan = jnp.repeat(weight.T, group_width, axis=1)
     width = chans // block
     wire = bf16
     vmem = pl.BlockSpec(memory_space=pltpu.VMEM)
-    anywhere = pl.BlockSpec(memory_space=pl.ANY)
+    hbm = pl.BlockSpec(memory_space=pltpu.HBM)
     dma = pltpu.SemaphoreType.DMA
     return pl.pallas_call(
         functools.partial(kernel, (ctx_count, head_count, block, reach)),
         out_shape=jax.ShapeDtypeStruct((tok, chans), bf16),
-        in_specs=[pl.BlockSpec(memory_space=pltpu.SMEM), anywhere, anywhere, anywhere] + [vmem] * 5,
-        out_specs=anywhere,
+        in_specs=[pl.BlockSpec(memory_space=pltpu.SMEM), hbm, hbm, hbm, vmem, vmem, vmem],
+        out_specs=hbm,
         scratch_shapes=[
             pltpu.VMEM((tok, chans), bf16), pltpu.VMEM((tok, chans), bf16),
             pltpu.VMEM((tok, chans), bf16), pltpu.VMEM((tok, chans), bf16),
             pltpu.VMEM((tok, chans), bf16), pltpu.VMEM((tok, chans), f32),
             pltpu.VMEM((tok, chans), bf16),
+            pltpu.VMEM((modes, chans), f32), pltpu.VMEM((modes, chans), f32),
+            pltpu.VMEM((1, chans), f32), pltpu.VMEM((1, chans), f32),
             pltpu.VMEM((block, modes, width), wire),
             pltpu.VMEM((block, modes, width), wire),
             pltpu.VMEM((block, modes, width), f32),
@@ -277,9 +303,8 @@
             dma((3,)), dma, dma((block - 1,)), dma((block - 1,)),
             dma((reach,)), dma((reach,)), dma((block - 1,)), dma((block - 1,)),
         ],
-        compiler_params=pltpu.CompilerParams(collective_id=0, has_side_effects=True,
-                                             vmem_limit_bytes=32 * 1024 * 1024),
-    )(doc_lengths, query_gate, key_gate, values, rate_rows, weight_rows, rate_chan, weight_chan, skip_gain.reshape(1, -1))
+        compiler_params=pltpu.CompilerParams(collective_id=0, has_side_effects=True),
+    )(doc_lengths, query_gate, key_gate, values, rate_mix.T, residue.T, skip_gain.reshape(1, -1))
 
 
 def solution(mesh):

time: 23.8 us -> 19.3 us (0.81)
  local copies, waits for them, and re-layouts: 8.07 us -> 2.29 us
  Pallas kernels: 14.5 us -> 16.8 us
  other arithmetic: 0.76 us -> 0 us
    reshape x4 -> x0, local copies, waits for them, and re-layouts: 4.28 us -> none  [the longest x1 2.78 us: shards(): weight_chan = jnp.repeat(weight.T, group_width, axis=1)]
    broadcast_in_dim x2 -> x0, local copies, waits for them, and re-layouts: 2.54 us -> none  [the longest x1 1.95 us: shards(): weight_chan = jnp.repeat(weight.T, group_width, axis=1)]
    pallas_call x1, Pallas kernels: 14.5 us -> 16.8 us  [shards(): pl.pallas_call(functools.partial(kernel, (ctx_count, head_count, block, r...]
    unnamed x11 -> x1, local copies, waits for them, and re-layouts: 1 us -> 2.29 us
    transpose x1 -> x0, other arithmetic: 0.76 us -> none  [shards(): rate_chan = jnp.repeat(rate.T, group_width, axis=1)]
where the time goes in v2:
time: 19.3 us; the launch traced here: 19.1 us
  Pallas kernels  16.8 us (87%)
  local copies, waits for them, and re-layouts  2.29 us (12%)
    pallas_call x1, Pallas kernels, shards(): pl.pallas_call(functools.partial(kernel, (ctx_count, head_count, block, r...  16.8 us
    unnamed x1, local copies, waits for them, and re-layouts  2.29 us

profile of v2, /device:TPU:25, one launch (start us, length us, event | category | flops | bytes accessed | tf_op | source)
XLA Modules:
  0.0 19.1 jit_solution(18383897637678269472)
XLA Ops:
  0.0 16.8 %shard_map.73 = bf16[128,4096]{1,0:T(8,128)(2,1)} custom-call(s32[16]{0:T(128)} %lengths.1, bf16[128,4096]{1,0:T(8,128)(2,1)} %q_hbm.1, bf16[128,4096]{1,0:T(8,128)(2,1)} %k_hbm.1, bf16[128,4096]{1,0:T(8,128)(2,1)} %v_hbm.1, f32[8,512]{1,0:T(8,128)} %bitcast.3, f32[8,512]{1,0:T(8,128)} %bitcast.4, f32[1,4096]{1,0:T(1,128)} %bitcast.5), custom_call_target="tpu_custom_call" | custom-call | tf_op jit(solution)/shard_map/pallas_call | solution.py:284
  16.8 2.3 %copy.9 = bf16[128,4096]{1,0:T(8,128)(2,1)} copy(bf16[128,4096]{1,0:T(8,128)(2,1)} %shard_map.73) | data formatting | bytes 2097152

commit v3 on v2

v3 whole, which is shorter than its diff:
```python
import functools
import math

import jax
import jax.numpy as jnp
from jax import lax
from jax.experimental import pallas as pl
from jax.experimental.pallas import tpu as pltpu
from jax.sharding import PartitionSpec as P

LANES = 128
EARLY = 3
CUTS = (7, 10)
MESH = pl.DeviceIdType.MESH
f32 = jnp.float32
bf16 = jnp.bfloat16


def doc_start(tokens, ends):
    start = jnp.zeros_like(tokens)
    for end in ends:
        start = jnp.maximum(start, jnp.where(tokens >= end, end, 0))
    return start


def split_three(x):
    high = x.astype(bf16)
    rest = x - high.astype(f32)
    middle = rest.astype(bf16)
    low = (rest - middle.astype(f32)).astype(bf16)
    return [high, middle, low]


def kernel(cfg, lengths, k_hbm, v_hbm, rate_mix, residue, skip,
           inner_hbm, table_hbm, enter_hbm, k_buf, v_buf, mixed, inner, cross_table,
           chan_rate, chan_weight, rate_row, weight_row,
           state_buf, gather_buf, prefix_buf, factor_buf, reply_buf, exit_buf, far_buf,
           load_sem, inner_sem, table_sem, own_sem, send1, recv1, send2, recv2, send3, recv3):
    ctx_count, head_count, block, reach = cfg
    devices = ctx_count * head_count
    tok, chans = mixed.shape
    modes = chan_rate.shape[0]
    lane_blocks = chans // LANES
    per_slice = lane_blocks // block
    group_width = LANES * modes // LANES
    block_count = devices // block
    me = lax.axis_index("ctx") * head_count + lax.axis_index("head")
    zone, pos = me // block, me % block
    span = me * tok

    def where_is(index):
        return (index // head_count, index % head_count)

    width = chans // block

    def mate_of(s):
        mate, bit = 0, 1
        while bit < block:
            mine = (pos // bit) % 2
            mate = mate + (1 - mine if s & bit else mine) * bit
            bit *= 2
        return mate

    order = sorted(range(block), key=lambda s: (-(s & ~head_count).bit_count(), s == 0))
    mates = {s: mate_of(s) for s in order}
    loads = {}
    for s in order:
        cols = pl.ds(pl.multiple_of(mates[s] * width, width), width)
        loads[s] = [pltpu.make_async_copy(src.at[:, cols], dst.at[:, cols], load_sem.at[n, s])
                    for n, (src, dst) in enumerate(((k_hbm, k_buf), (v_hbm, v_buf)))]
        for load in loads[s]:
            load.start()

    barrier = pltpu.get_barrier_semaphore()
    for s in order:
        if s:
            pl.semaphore_signal(barrier, inc=1, device_id=where_is(zone * block + mates[s]), device_id_type=MESH)
    for k in range(1, reach + 1):
        @pl.when(zone + k < block_count)
        def _(k=k):
            pl.semaphore_signal(barrier, inc=1, device_id=where_is(me + k * block), device_id_type=MESH)

        @pl.when(zone >= k)
        def _(k=k):
            pl.semaphore_signal(barrier, inc=1, device_id=where_is(me - k * block), device_id_type=MESH)

    ends, total = [], jnp.int32(0)
    for n in range(lengths.shape[0]):
        total = total + lengths[n]
        ends.append(total)

    def start_of(token):
        return doc_start(jnp.full((modes, LANES), token, jnp.int32), ends)

    rows = lax.broadcasted_iota(jnp.int32, (tok, LANES), 0)
    gr = lax.broadcasted_iota(jnp.int32, (LANES, LANES), 0) // modes
    gc = lax.broadcasted_iota(jnp.int32, (LANES, LANES), 1) // group_width
    diagonal = gr == gc

    rate = jnp.exp(-math.log(30.0) - rate_mix[...] * math.log(float(devices * tok)))
    double = 2.0 * rate
    one_minus = jnp.where(double < 1e-2,
                          double * (1.0 - double * (0.5 - double * (1.0 / 6.0 - double / 24.0))),
                          1.0 - jnp.exp(-double))
    weight = residue[...] * jnp.sqrt(one_minus)
    stacked = jnp.concatenate([p.astype(f32) for p in split_three(rate) + split_three(weight)], axis=0).astype(bf16)
    spread_to = LANES * group_width
    onto = jnp.where(lax.broadcasted_iota(jnp.int32, (LANES, spread_to), 0)
                     == lax.broadcasted_iota(jnp.int32, (LANES, spread_to), 1) // group_width, 1.0, 0.0).astype(bf16)
    own = (lax.broadcasted_iota(jnp.int32, (modes, spread_to), 0)
           == lax.broadcasted_iota(jnp.int32, (modes, spread_to), 1) % modes)
    for n in range(rate.shape[1] // LANES):
        wide_table = jnp.dot(stacked[:, n * LANES:(n + 1) * LANES], onto, preferred_element_type=f32)
        parts = [wide_table[m * modes:(m + 1) * modes] for m in range(6)]
        cols = slice(n * spread_to, (n + 1) * spread_to)
        for m, (table, row) in enumerate(((chan_rate, rate_row), (chan_weight, weight_row))):
            value = parts[3 * m] + (parts[3 * m + 1] + parts[3 * m + 2])
            table[:, cols] = value
            row[:, cols] = jnp.sum(jnp.where(own, value, 0.0), axis=0, keepdims=True)

    tail_start = start_of(span + tok - 1)[:1] - span
    tail = rows >= tail_start
    left = (tok - 1 - rows).astype(f32)

    expected = block - 1
    for k in range(1, reach + 1):
        expected = expected + jnp.where(zone + k < block_count, 1, 0) + jnp.where(zone >= k, 1, 0)

    def local(s):
        for load in loads[s]:
            load.wait()
        for i in range(per_slice):
            cols = pl.ds(pl.multiple_of(mates[s] * width + i * LANES, LANES), LANES)
            x = k_buf[:, cols] * v_buf[:, cols]
            mixed[:, cols] = x
            rate = rate_row[:, cols]
            table = jnp.where(tail, jnp.exp(-rate * left), 0.0).astype(bf16)
            full = lax.dot_general(table, x, (((0,), (0,)), ((), ())), preferred_element_type=f32)
            full = jnp.where(diagonal, full, 0.0)
            state = jnp.sum(full.reshape(LANES // modes, modes, LANES), axis=0)
            state_buf[mates[s], :, i * LANES:(i + 1) * LANES] = state.astype(state_buf.dtype)

    first = {s: pltpu.make_async_remote_copy(
        src_ref=state_buf.at[mates[s]], dst_ref=gather_buf.at[pos],
        send_sem=send1.at[s - 1], recv_sem=recv1.at[s - 1],
        device_id=where_is(zone * block + mates[s]), device_id_type=MESH) for s in order if s}

    early = order[:EARLY]
    for s in early:
        local(s)
    pl.semaphore_wait(barrier, expected)
    for s in early:
        first[s].start()
    for s in order[EARLY:]:
        local(s)
        if s:
            first[s].start()
    gather_buf[pos] = state_buf[pos]

    row_tok = span + rows
    row_start = doc_start(row_tok, ends) - span
    lane_iota = lax.broadcasted_iota(jnp.int32, (tok, tok), 1)
    row_iota = lax.broadcasted_iota(jnp.int32, (tok, tok), 0)
    mask = jnp.where((lane_iota >= row_start[:, :1]) & (lane_iota <= row_iota), 1.0, 0.0).astype(bf16)
    linked = row_start < 0
    ahead = (rows + 1).astype(f32)

    wide = 2 * LANES
    wide_blocks = chans // wide
    eights = lax.broadcasted_iota(jnp.int32, (8, wide), 0).astype(f32)

    def conv(b, _):
        cols = pl.ds(pl.multiple_of(b * wide, wide), wide)
        x = mixed[:, cols].astype(f32)
        total = skip[:, cols] * x
        for r in range(modes):
            rate = chan_rate[r:r + 1, cols]
            up = jnp.exp(rate * eights)
            down = chan_weight[r:r + 1, cols] * jnp.exp(-rate * eights)
            up_step = jnp.broadcast_to(jnp.exp(8.0 * rate), up.shape)
            down_step = jnp.broadcast_to(jnp.exp(-8.0 * rate), up.shape)
            ups, downs = [], []
            for _p in range(tok // 8):
                ups.append(up)
                downs.append(down)
                up, down = up * up_step, down * down_step
            scaled = (x * jnp.concatenate(ups, axis=0)).astype(bf16)
            summed = jnp.dot(mask, scaled, preferred_element_type=f32)
            total = total + jnp.concatenate(downs, axis=0) * summed
        inner[:, cols] = total.astype(inner.dtype)
        pltpu.make_async_copy(inner.at[:, cols], inner_hbm.at[:, cols], inner_sem.at[b]).start()
        return 0

    def entering_table(b, _):
        cols = pl.ds(pl.multiple_of(b * LANES, LANES), LANES)
        rate = rate_row[:, cols]
        weight = weight_row[:, cols]
        cross_table[:, cols] = jnp.where(linked, weight * jnp.exp(-rate * ahead), 0.0).astype(bf16)
        return 0

    cut1, cut2 = wide_blocks * CUTS[0] // 16, wide_blocks * CUTS[1] // 16
    lax.fori_loop(0, cut1, conv, 0)
    lax.fori_loop(0, lane_blocks, entering_table, 0, unroll=4)
    table_store = pltpu.make_async_copy(cross_table, table_hbm, table_sem)
    table_store.start()

    slice_rate = chan_rate[:, pl.ds(pl.multiple_of(pos * width, width), width)]
    decay = jnp.exp(-slice_rate * float(tok))

    def repeat_lanes(row):
        return jnp.concatenate([row] * (width // LANES), axis=1)

    def keep_of(index):
        crossing = start_of(index * tok + tok - 1) < index * tok
        return repeat_lanes(jnp.where(crossing, 1.0, 0.0))

    keeps = [keep_of(zone * block + e) * decay for e in range(block)]
    last_start = start_of(jnp.maximum(zone * block * tok - 1, 0))

    for copy in first.values():
        copy.wait()
    carry = jnp.zeros(slice_rate.shape, f32)
    factor = jnp.ones(slice_rate.shape, f32)
    for e in range(block):
        prefix_buf[e] = carry
        factor_buf[e] = factor
        step = keeps[e]
        carry = step * carry + gather_buf[e].astype(f32)
        factor = step * factor
    exit_buf[...] = carry.astype(exit_buf.dtype)

    def onward(k):
        return pltpu.make_async_remote_copy(
            src_ref=exit_buf, dst_ref=far_buf.at[k - 1],
            send_sem=send2.at[k - 1], recv_sem=recv2.at[k - 1],
            device_id=where_is(me + k * block), device_id_type=MESH)

    for k in range(1, reach + 1):
        @pl.when(zone + k < block_count)
        def _(k=k):
            onward(k).start()

    lax.fori_loop(cut1, cut2, conv, 0)

    for k in range(1, reach + 1):
        @pl.when(zone >= k)
        def _(k=k):
            onward(k).wait_recv()

        @pl.when(zone < k)
        def _(k=k):
            far_buf[k - 1] = jnp.zeros(far_buf.shape[1:], far_buf.dtype)

    far = jnp.zeros(slice_rate.shape, f32)
    for k in range(1, reach + 1):
        same = (last_start < (zone - k + 1) * block * tok)
        flag = repeat_lanes(jnp.where(same, 1.0, 0.0))
        scale = flag * jnp.exp(-slice_rate * float(tok * block * (k - 1)))
        far = far + scale * far_buf[k - 1].astype(f32)
    last = {s: pltpu.make_async_remote_copy(
        src_ref=reply_buf.at[mates[s]], dst_ref=enter_hbm.at[pos],
        send_sem=send3.at[s - 1], recv_sem=recv3.at[s - 1],
        device_id=where_is(zone * block + mates[s]), device_id_type=MESH) for s in order if s}
    for s in order:
        reply_buf[mates[s]] = (prefix_buf[mates[s]] + factor_buf[mates[s]] * far).astype(reply_buf.dtype)
        if s:
            last[s].start()
    own_copy = pltpu.make_async_copy(reply_buf.at[pos], enter_hbm.at[pos], own_sem)
    own_copy.start()

    lax.fori_loop(cut2, wide_blocks, conv, 0)

    for k in range(1, reach + 1):
        @pl.when(zone + k < block_count)
        def _(k=k):
            onward(k).wait_send()
    table_store.wait()

    def stored(b, _):
        cols = pl.ds(pl.multiple_of(b * wide, wide), wide)
        pltpu.make_async_copy(inner.at[:, cols], inner_hbm.at[:, cols], inner_sem.at[b]).wait()
        return 0

    lax.fori_loop(0, wide_blocks, stored, 0)
    own_copy.wait()
    for copy in last.values():
        copy.wait()


def finish_kernel(q_hbm, inner_hbm, table_hbm, enter_hbm, out_hbm,
                  q_buf, inner, table, enter, out_buf, enter_sem, load_sem, store_sem):
    tok, chans = q_buf.shape
    block, modes, width = enter.shape
    group_width = modes
    entering = pltpu.make_async_copy(enter_hbm, enter, enter_sem)
    entering.start()
    loads = []
    for e in range(block):
        cols = slice(e * width, (e + 1) * width)
        loads.append([pltpu.make_async_copy(src.at[:, cols], dst.at[:, cols], load_sem.at[n, e])
                      for n, (src, dst) in enumerate(((q_hbm, q_buf), (inner_hbm, inner), (table_hbm, table)))])
        for load in loads[e]:
            load.start()
    diagonal = (lax.broadcasted_iota(jnp.int32, (LANES, LANES), 0) // modes
                == lax.broadcasted_iota(jnp.int32, (LANES, LANES), 1) // group_width)
    entering.wait()
    stores = []
    for e in range(block):
        for load in loads[e]:
            load.wait()
        for i in range(width // LANES):
            cols = slice(e * width + i * LANES, e * width + (i + 1) * LANES)
            state = enter[e, :, i * LANES:(i + 1) * LANES].astype(f32)
            spread = jnp.where(diagonal, jnp.concatenate([state] * (LANES // modes), axis=0), 0.0).astype(bf16)
            cross = jnp.dot(table[:, cols], spread, preferred_element_type=f32)
            smoothed = (inner[:, cols].astype(f32) + cross).astype(bf16)
            out_buf[:, cols] = q_buf[:, cols] * smoothed
        cols = slice(e * width, (e + 1) * width)
        stores.append(pltpu.make_async_copy(out_buf.at[:, cols], out_hbm.at[:, cols], store_sem.at[e]))
        stores[e].start()
    for store in stores:
        store.wait()


def shards(query_gate, key_gate, values, rate_mix, residue, skip_gain, doc_lengths):
    ctx_count = lax.axis_size("ctx")
    head_count = lax.axis_size("head")
    devices = ctx_count * head_count
    tok, chans = query_gate.shape
    groups, modes = rate_mix.shape
    group_width = chans // groups
    total_tokens = tok * devices
    longest = total_tokens // 4
    block = min(devices // 4, chans // (4 * LANES))
    reach = -(-longest // (tok * block))
    width = chans // block
    wire = bf16
    vmem = pl.BlockSpec(memory_space=pltpu.VMEM)
    hbm = pl.BlockSpec(memory_space=pltpu.HBM)
    dma = pltpu.SemaphoreType.DMA
    whole = pltpu.VMEM((tok, chans), bf16)
    slices = pltpu.VMEM((block, modes, width), wire)
    inner, table, enter = pl.pallas_call(
        functools.partial(kernel, (ctx_count, head_count, block, reach)),
        out_shape=(jax.ShapeDtypeStruct((tok, chans), bf16), jax.ShapeDtypeStruct((tok, chans), bf16),
                   jax.ShapeDtypeStruct((block, modes, width), wire)),
        in_specs=[pl.BlockSpec(memory_space=pltpu.SMEM), hbm, hbm, vmem, vmem, vmem],
        out_specs=(hbm, hbm, hbm),
        scratch_shapes=[
            whole, whole, whole, whole, whole,
            pltpu.VMEM((modes, chans), f32), pltpu.VMEM((modes, chans), f32),
            pltpu.VMEM((1, chans), f32), pltpu.VMEM((1, chans), f32),
            slices, slices,
            pltpu.VMEM((block, modes, width), f32), pltpu.VMEM((block, modes, width), f32),
            slices,
            pltpu.VMEM((modes, width), wire),
            pltpu.VMEM((reach, modes, width), wire),
            dma((2, block)), dma((chans // (2 * LANES),)), dma, dma,
            dma((block - 1,)), dma((block - 1,)),
            dma((reach,)), dma((reach,)), dma((block - 1,)), dma((block - 1,)),
        ],
        compiler_params=pltpu.CompilerParams(collective_id=0, has_side_effects=True),
    )(doc_lengths, key_gate, values, rate_mix.T, residue.T, skip_gain.reshape(1, -1))
    return pl.pallas_call(
        finish_kernel,
        out_shape=jax.ShapeDtypeStruct((tok, chans), bf16),
        in_specs=[hbm] * 4,
        out_specs=hbm,
        scratch_shapes=[whole, whole, whole, slices, whole, dma, dma((3, block)), dma((block,))],
    )(query_gate, inner, table, enter)


def solution(mesh):
    spans = P(("ctx", "head"), None)
    return jax.shard_map(
        shards,
        mesh=mesh,
        in_specs=(spans, spans, spans, P(), P(), P(), P()),
        out_specs=spans,
        check_vma=False,
    )
```

time: 19.3 us -> 18.7 us (0.969)
  local copies, waits for them, and re-layouts: 2.29 us -> 0 us
  Pallas kernels: 16.8 us -> 18.4 us
    pallas_call x0 -> x1, Pallas kernels: none -> 4.26 us  [shards(): pl.pallas_call(finish_kernel, out_shape=jax.ShapeDtypeStruct((tok, chans)...]
    pallas_call x1, Pallas kernels: 16.8 us -> 14.1 us  [shards(): pl.pallas_call(functools.partial(kernel, (ctx_count, head_count, block, r...]
    unnamed x1 -> x0, local copies, waits for them, and re-layouts: 2.29 us -> none
where the time goes in v3:
time: 18.7 us; the launch traced here: 18.4 us
  Pallas kernels  18.4 us (98%)
    pallas_call x1, Pallas kernels, shards(): pl.pallas_call(functools.partial(kernel, (ctx_count, head_count, block, r...  14.1 us
    pallas_call x1, Pallas kernels, shards(): pl.pallas_call(finish_kernel, out_shape=jax.ShapeDtypeStruct((tok, chans)...  4.26 us

profile of v3, /device:TPU:25, one launch (start us, length us, event | category | flops | bytes accessed | tf_op | source)
XLA Modules:
  0.0 18.4 jit_solution(15868354941349404131)
XLA Ops:
  0.0 14.1 %shard_map.73 = (bf16[128,4096]{1,0:T(8,128)(2,1)}, bf16[128,4096]{1,0:T(8,128)(2,1)}, bf16[8,8,512]{2,1,0:T(8,128)(2,1)}) custom-call(s32[16]{0:T(128)} %lengths.1, bf16[128,4096]{1,0:T(8,128)(2,1)} %k_hbm.1, bf16[128,4096]{1,0:T(8,128)(2,1)} %v_hbm.1, f32[8,512]{1,0:T(8,128)} %bitcast.3, f32[8,512]{1,0:T(8,128)} %bitcast.4, f32[1,4096]{1,0:T(1,128)} %bitcast.5), custom_call_target="tpu_custom_call" | custom-call | tf_op jit(solution)/shard_map/pallas_call | solution.py:343
  14.1 4.3 %shard_map.74 = bf16[128,4096]{1,0:T(8,128)(2,1)} custom-call(bf16[128,4096]{1,0:T(8,128)(2,1)} %q_hbm.1, bf16[128,4096]{1,0:T(8,128)(2,1)} %get-tuple-element.8.inner_hbm, bf16[128,4096]{1,0:T(8,128)(2,1)} %get-tuple-element.9.table_hbm, bf16[8,8,512]{2,1,0:T(8,128)(2,1)} %get-tuple-element.10.enter_hbm), custom_call_target="tpu_custom_call" | custom-call | tf_op jit(solution)/shard_map/pallas_call | solution.py:364

commit v4 on v3

--- a/solution.py
+++ b/solution.py
@@ -31,11 +31,11 @@
     return [high, middle, low]
 
 
-def kernel(cfg, lengths, k_hbm, v_hbm, rate_mix, residue, skip,
-           inner_hbm, table_hbm, enter_hbm, k_buf, v_buf, mixed, inner, cross_table,
+def kernel(cfg, lengths, q_hbm, k_hbm, v_hbm, rate_mix, residue, skip,
+           out_buf, q_buf, k_buf, v_buf, mixed, inner, cross_table,
            chan_rate, chan_weight, rate_row, weight_row,
-           state_buf, gather_buf, prefix_buf, factor_buf, reply_buf, exit_buf, far_buf,
-           load_sem, inner_sem, table_sem, own_sem, send1, recv1, send2, recv2, send3, recv3):
+           state_buf, gather_buf, prefix_buf, factor_buf, reply_buf, enter_buf, exit_buf, far_buf,
+           load_sem, q_sem, send1, recv1, send2, recv2, send3, recv3):
     ctx_count, head_count, block, reach = cfg
     devices = ctx_count * head_count
     tok, chans = mixed.shape
@@ -70,6 +70,8 @@
                     for n, (src, dst) in enumerate(((k_hbm, k_buf), (v_hbm, v_buf)))]
         for load in loads[s]:
             load.start()
+    q_load = pltpu.make_async_copy(q_hbm, q_buf, q_sem)
+    q_load.start()
 
     barrier = pltpu.get_barrier_semaphore()
     for s in order:
@@ -187,8 +189,7 @@
             scaled = (x * jnp.concatenate(ups, axis=0)).astype(bf16)
             summed = jnp.dot(mask, scaled, preferred_element_type=f32)
             total = total + jnp.concatenate(downs, axis=0) * summed
-        inner[:, cols] = total.astype(inner.dtype)
-        pltpu.make_async_copy(inner.at[:, cols], inner_hbm.at[:, cols], inner_sem.at[b]).start()
+        inner[:, cols] = total
         return 0
 
     def entering_table(b, _):
@@ -201,8 +202,6 @@
     cut1, cut2 = wide_blocks * CUTS[0] // 16, wide_blocks * CUTS[1] // 16
     lax.fori_loop(0, cut1, conv, 0)
     lax.fori_loop(0, lane_blocks, entering_table, 0, unroll=4)
-    table_store = pltpu.make_async_copy(cross_table, table_hbm, table_sem)
-    table_store.start()
 
     slice_rate = chan_rate[:, pl.ds(pl.multiple_of(pos * width, width), width)]
     decay = jnp.exp(-slice_rate * float(tok))
@@ -258,15 +257,14 @@
         scale = flag * jnp.exp(-slice_rate * float(tok * block * (k - 1)))
         far = far + scale * far_buf[k - 1].astype(f32)
     last = {s: pltpu.make_async_remote_copy(
-        src_ref=reply_buf.at[mates[s]], dst_ref=enter_hbm.at[pos],
+        src_ref=reply_buf.at[mates[s]], dst_ref=enter_buf.at[pos],
         send_sem=send3.at[s - 1], recv_sem=recv3.at[s - 1],
         device_id=where_is(zone * block + mates[s]), device_id_type=MESH) for s in order if s}
     for s in order:
         reply_buf[mates[s]] = (prefix_buf[mates[s]] + factor_buf[mates[s]] * far).astype(reply_buf.dtype)
         if s:
             last[s].start()
-    own_copy = pltpu.make_async_copy(reply_buf.at[pos], enter_hbm.at[pos], own_sem)
-    own_copy.start()
+    enter_buf[pos] = reply_buf[pos]
 
     lax.fori_loop(cut2, wide_blocks, conv, 0)
 
@@ -274,52 +272,20 @@
         @pl.when(zone + k < block_count)
         def _(k=k):
             onward(k).wait_send()
-    table_store.wait()
-
-    def stored(b, _):
-        cols = pl.ds(pl.multiple_of(b * wide, wide), wide)
-        pltpu.make_async_copy(inner.at[:, cols], inner_hbm.at[:, cols], inner_sem.at[b]).wait()
-        return 0
-
-    lax.fori_loop(0, wide_blocks, stored, 0)
-    own_copy.wait()
+    q_load.wait()
     for copy in last.values():
         copy.wait()
 
-
-def finish_kernel(q_hbm, inner_hbm, table_hbm, enter_hbm, out_hbm,
-                  q_buf, inner, table, enter, out_buf, enter_sem, load_sem, store_sem):
-    tok, chans = q_buf.shape
-    block, modes, width = enter.shape
-    group_width = modes
-    entering = pltpu.make_async_copy(enter_hbm, enter, enter_sem)
-    entering.start()
-    loads = []
-    for e in range(block):
-        cols = slice(e * width, (e + 1) * width)
-        loads.append([pltpu.make_async_copy(src.at[:, cols], dst.at[:, cols], load_sem.at[n, e])
-                      for n, (src, dst) in enumerate(((q_hbm, q_buf), (inner_hbm, inner), (table_hbm, table)))])
-        for load in loads[e]:
-            load.start()
-    diagonal = (lax.broadcasted_iota(jnp.int32, (LANES, LANES), 0) // modes
-                == lax.broadcasted_iota(jnp.int32, (LANES, LANES), 1) // group_width)
-    entering.wait()
-    stores = []
-    for e in range(block):
-        for load in loads[e]:
-            load.wait()
-        for i in range(width // LANES):
-            cols = slice(e * width + i * LANES, e * width + (i + 1) * LANES)
-            state = enter[e, :, i * LANES:(i + 1) * LANES].astype(f32)
-            spread = jnp.where(diagonal, jnp.concatenate([state] * (LANES // modes), axis=0), 0.0).astype(bf16)
-            cross = jnp.dot(table[:, cols], spread, preferred_element_type=f32)
-            smoothed = (inner[:, cols].astype(f32) + cross).astype(bf16)
-            out_buf[:, cols] = q_buf[:, cols] * smoothed
-        cols = slice(e * width, (e + 1) * width)
-        stores.append(pltpu.make_async_copy(out_buf.at[:, cols], out_hbm.at[:, cols], store_sem.at[e]))
-        stores[e].start()
-    for store in stores:
-        store.wait()
+    def finish(b, _):
+        cols = pl.ds(pl.multiple_of(b * LANES, LANES), LANES)
+        state = enter_buf[b // per_slice, :, pl.ds(pl.multiple_of((b % per_slice) * LANES, LANES), LANES)].astype(f32)
+        spread = jnp.where(diagonal, jnp.concatenate([state] * (LANES // modes), axis=0), 0.0).astype(bf16)
+        cross = jnp.dot(cross_table[:, cols], spread, preferred_element_type=f32)
+        smoothed = (inner[:, cols] + cross).astype(bf16)
+        out_buf[:, cols] = q_buf[:, cols] * smoothed
+        return 0
+
+    lax.fori_loop(0, lane_blocks, finish, 0, unroll=4)
 
 
 def shards(query_gate, key_gate, values, rate_mix, residue, skip_gain, doc_lengths):
@@ -340,34 +306,31 @@
     dma = pltpu.SemaphoreType.DMA
     whole = pltpu.VMEM((tok, chans), bf16)
     slices = pltpu.VMEM((block, modes, width), wire)
-    inner, table, enter = pl.pallas_call(
+    def pin(x):
+        return pltpu.with_memory_space_constraint(x, pltpu.HBM)
+
+    return pl.pallas_call(
         functools.partial(kernel, (ctx_count, head_count, block, reach)),
-        out_shape=(jax.ShapeDtypeStruct((tok, chans), bf16), jax.ShapeDtypeStruct((tok, chans), bf16),
-                   jax.ShapeDtypeStruct((block, modes, width), wire)),
-        in_specs=[pl.BlockSpec(memory_space=pltpu.SMEM), hbm, hbm, vmem, vmem, vmem],
-        out_specs=(hbm, hbm, hbm),
+        out_shape=jax.ShapeDtypeStruct((tok, chans), bf16),
+        in_specs=[pl.BlockSpec(memory_space=pltpu.SMEM), hbm, hbm, hbm, vmem, vmem, vmem],
+        out_specs=vmem,
         scratch_shapes=[
-            whole, whole, whole, whole, whole,
+            whole, whole, whole, whole, pltpu.VMEM((tok, chans), f32), whole,
             pltpu.VMEM((modes, chans), f32), pltpu.VMEM((modes, chans), f32),
             pltpu.VMEM((1, chans), f32), pltpu.VMEM((1, chans), f32),
             slices, slices,
             pltpu.VMEM((block, modes, width), f32), pltpu.VMEM((block, modes, width), f32),
-            slices,
+            slices, slices,
             pltpu.VMEM((modes, width), wire),
             pltpu.VMEM((reach, modes, width), wire),
-            dma((2, block)), dma((chans // (2 * LANES),)), dma, dma,
+            dma((2, block)), dma,
             dma((block - 1,)), dma((block - 1,)),
             dma((reach,)), dma((reach,)), dma((block - 1,)), dma((block - 1,)),
         ],
-        compiler_params=pltpu.CompilerParams(collective_id=0, has_side_effects=True),
-    )(doc_lengths, key_gate, values, rate_mix.T, residue.T, skip_gain.reshape(1, -1))
-    return pl.pallas_call(
-        finish_kernel,
-        out_shape=jax.ShapeDtypeStruct((tok, chans), bf16),
-        in_specs=[hbm] * 4,
-        out_specs=hbm,
-        scratch_shapes=[whole, whole, whole, slices, whole, dma, dma((3, block)), dma((block,))],
-    )(query_gate, inner, table, enter)
+        compiler_params=pltpu.CompilerParams(collective_id=0, has_side_effects=True,
+                                             vmem_limit_bytes=32 * 1024 * 1024),
+    )(pin(doc_lengths), pin(query_gate), pin(key_gate), pin(values),
+      pin(rate_mix.T), pin(residue.T), pin(skip_gain.reshape(1, -1)))
 
 
 def solution(mesh):

time: 18.7 us -> 17.1 us (0.914)
  Pallas kernels: 18.4 us -> 15.8 us
  local copies, waits for them, and re-layouts: 0 us -> 0.97 us
    pallas_call x1 -> x0, Pallas kernels: 4.26 us -> none  [shards(): pl.pallas_call(finish_kernel, out_shape=jax.ShapeDtypeStruct((tok, chans)...]
    pallas_call x1, Pallas kernels: 14.1 us -> 15.8 us  [shards(): pl.pallas_call(functools.partial(kernel, (ctx_count, head_count, block, r...]
    unnamed x0 -> x1, local copies, waits for them, and re-layouts: none -> 0.97 us
where the time goes in v4:
time: 17.1 us; the launch traced here: 16.8 us
  Pallas kernels  15.8 us (92%)
  local copies, waits for them, and re-layouts  0.97 us (6%)
    pallas_call x1, Pallas kernels, shards(): pl.pallas_call(functools.partial(kernel, (ctx_count, head_count, block, r...  15.8 us
    unnamed x1, local copies, waits for them, and re-layouts  0.97 us

profile of v4, /device:TPU:25, one launch (start us, length us, event | category | flops | bytes accessed | tf_op | source)
XLA Modules:
  0.0 16.8 jit_solution(14107239147073023952)
XLA Ops:
  0.0 15.8 %shard_map.73 = bf16[128,4096]{1,0:T(8,128)(2,1)S(1)} custom-call(s32[16]{0:T(128)} %lengths.1, bf16[128,4096]{1,0:T(8,128)(2,1)} %q_hbm.1, bf16[128,4096]{1,0:T(8,128)(2,1)} %k_hbm.1, bf16[128,4096]{1,0:T(8,128)(2,1)} %v_hbm.1, f32[8,512]{1,0:T(8,128)} %bitcast.3, f32[8,512]{1,0:T(8,128)} %bitcast.4, f32[1,4096]{1,0:T(1,128)} %bitcast.5), custom_call_target="tpu_custom_call" | custom-call | tf_op jit(solution)/shard_map/pallas_call | solution.py:312
  15.8 1.0 %copy.9 = bf16[128,4096]{1,0:T(8,128)(2,1)} copy(bf16[128,4096]{1,0:T(8,128)(2,1)S(1)} %shard_map.73) | data formatting | bytes 2097152

commit v5 on v4

--- a/solution.py
+++ b/solution.py
@@ -10,7 +10,7 @@
 
 LANES = 128
 EARLY = 3
-CUTS = (7, 10)
+CUTS = (4, 6)
 MESH = pl.DeviceIdType.MESH
 f32 = jnp.float32
 bf16 = jnp.bfloat16
@@ -31,11 +31,11 @@
     return [high, middle, low]
 
 
-def kernel(cfg, lengths, q_hbm, k_hbm, v_hbm, rate_mix, residue, skip,
+def kernel(cfg, lengths_hbm, q_hbm, k_hbm, v_hbm, rate_hbm, residue_hbm, skip_hbm,
            out_buf, q_buf, k_buf, v_buf, mixed, inner, cross_table,
            chan_rate, chan_weight, rate_row, weight_row,
            state_buf, gather_buf, prefix_buf, factor_buf, reply_buf, enter_buf, exit_buf, far_buf,
-           load_sem, q_sem, send1, recv1, send2, recv2, send3, recv3):
+           lengths, rate_mix, residue, skip, small_sem, load_sem, q_sem, send1, recv1, send2, recv2, send3, recv3):
     ctx_count, head_count, block, reach = cfg
     devices = ctx_count * head_count
     tok, chans = mixed.shape
@@ -53,6 +53,11 @@
 
     width = chans // block
 
+    small = [pltpu.make_async_copy(src, dst, small_sem.at[n]) for n, (src, dst) in enumerate(
+        ((rate_hbm, rate_mix), (residue_hbm, residue), (lengths_hbm, lengths), (skip_hbm, skip)))]
+    for copy in small:
+        copy.start()
+
     def mate_of(s):
         mate, bit = 0, 1
         while bit < block:
@@ -86,19 +91,13 @@
         def _(k=k):
             pl.semaphore_signal(barrier, inc=1, device_id=where_is(me - k * block), device_id_type=MESH)
 
-    ends, total = [], jnp.int32(0)
-    for n in range(lengths.shape[0]):
-        total = total + lengths[n]
-        ends.append(total)
-
-    def start_of(token):
-        return doc_start(jnp.full((modes, LANES), token, jnp.int32), ends)
-
     rows = lax.broadcasted_iota(jnp.int32, (tok, LANES), 0)
     gr = lax.broadcasted_iota(jnp.int32, (LANES, LANES), 0) // modes
     gc = lax.broadcasted_iota(jnp.int32, (LANES, LANES), 1) // group_width
     diagonal = gr == gc
 
+    small[0].wait()
+    small[1].wait()
     rate = jnp.exp(-math.log(30.0) - rate_mix[...] * math.log(float(devices * tok)))
     double = 2.0 * rate
     one_minus = jnp.where(double < 1e-2,
@@ -120,6 +119,16 @@
             table[:, cols] = value
             row[:, cols] = jnp.sum(jnp.where(own, value, 0.0), axis=0, keepdims=True)
 
+    small[2].wait()
+    small[3].wait()
+    ends, total = [], jnp.int32(0)
+    for n in range(lengths.shape[0]):
+        total = total + lengths[n]
+        ends.append(total)
+
+    def start_of(token):
+        return doc_start(jnp.full((modes, LANES), token, jnp.int32), ends)
+
     tail_start = start_of(span + tok - 1)[:1] - span
     tail = rows >= tail_start
     left = (tok - 1 - rows).astype(f32)
@@ -285,7 +294,7 @@
         out_buf[:, cols] = q_buf[:, cols] * smoothed
         return 0
 
-    lax.fori_loop(0, lane_blocks, finish, 0, unroll=4)
+    lax.fori_loop(0, lane_blocks, finish, 0, unroll=16)
 
 
 def shards(query_gate, key_gate, values, rate_mix, residue, skip_gain, doc_lengths):
@@ -312,7 +321,7 @@
     return pl.pallas_call(
         functools.partial(kernel, (ctx_count, head_count, block, reach)),
         out_shape=jax.ShapeDtypeStruct((tok, chans), bf16),
-        in_specs=[pl.BlockSpec(memory_space=pltpu.SMEM), hbm, hbm, hbm, vmem, vmem, vmem],
+        in_specs=[hbm] * 7,
         out_specs=vmem,
         scratch_shapes=[
             whole, whole, whole, whole, pltpu.VMEM((tok, chans), f32), whole,
@@ -323,6 +332,8 @@
             slices, slices,
             pltpu.VMEM((modes, width), wire),
             pltpu.VMEM((reach, modes, width), wire),
+            pltpu.SMEM(doc_lengths.shape, jnp.int32), pltpu.VMEM((modes, groups), f32),
+            pltpu.VMEM((modes, groups), f32), pltpu.VMEM((1, chans), f32), dma((4,)),
             dma((2, block)), dma,
             dma((block - 1,)), dma((block - 1,)),
             dma((reach,)), dma((reach,)), dma((block - 1,)), dma((block - 1,)),

time: 17.1 us -> 14.7 us (0.86)
  Pallas kernels: 15.8 us -> 13.5 us
    pallas_call x1, Pallas kernels: 15.8 us -> 13.5 us  [shards(): pl.pallas_call(functools.partial(kernel, (ctx_count, head_count, block, r...]
where the time goes in v5:
time: 14.7 us; the launch traced here: 14.5 us
  Pallas kernels  13.5 us (92%)
  local copies, waits for them, and re-layouts  0.97 us (7%)
    pallas_call x1, Pallas kernels, shards(): pl.pallas_call(functools.partial(kernel, (ctx_count, head_count, block, r...  13.5 us
    unnamed x1, local copies, waits for them, and re-layouts  0.97 us

profile of v5, /device:TPU:25, one launch (start us, length us, event | category | flops | bytes accessed | tf_op | source)
XLA Modules:
  0.0 14.5 jit_solution(10568017145749268790)
XLA Ops:
  0.0 13.5 %shard_map.73 = bf16[128,4096]{1,0:T(8,128)(2,1)S(1)} custom-call(s32[16]{0:T(128)} %lengths_hbm.1, bf16[128,4096]{1,0:T(8,128)(2,1)} %q_hbm.1, bf16[128,4096]{1,0:T(8,128)(2,1)} %k_hbm.1, bf16[128,4096]{1,0:T(8,128)(2,1)} %v_hbm.1, f32[8,512]{1,0:T(8,128)} %bitcast.3, f32[8,512]{1,0:T(8,128)} %bitcast.4, f32[1,4096]{1,0:T(1,128)} %bitcast.5), custom_call_target="tpu_custom_call" | custom-call | tf_op jit(solution)/shard_map/pallas_call | solution.py:321
  13.5 1.0 %copy.9 = bf16[128,4096]{1,0:T(8,128)(2,1)} copy(bf16[128,4096]{1,0:T(8,128)(2,1)S(1)} %shard_map.73) | data formatting | bytes 2097152
